TPU v7x, 512 devices: a whole 4x8x8 slice. The times are simulated.
512 devices in a mesh: exp: 32 (over x_lo, z, core), ccd: 16 (over x_hi, y).
Axes of the slice: x: 4 (x_hi: 2, x_lo: 2; x = x_hi * 2 + x_lo), y: 8, z: 8, core: 2. Of those that a mesh axis runs over, the one named last changes fastest.
Arguments:
- pixels: bfloat16 [32, 16000, 4, 128], P('exp', 'ccd'), may hold values from -24 to 24
- psf_proj: bfloat16 [32, 100, 2160], P('ccd'), may hold values from -0.5 to 0.5
- resolution: float32 [800, 11, 512], P('ccd', None, 'exp'), may hold values from 0.02 to 0.16
- basis: float32 [10, 528], replicated, may hold values from -4 to 4
- sky_fibres: int32 [96], replicated, may hold values from 0 to 799, as said below
- fibre_slot: int32 [800], P('ccd'), may hold values from 0 to 799, as said below
- band_shift: int32 [800], P('ccd'), may hold values from -3 to 3
Outputs:
- sky_subtracted: float32 [32, 800, 512], P(None, 'ccd', 'exp')
- noise_rms: float32 [800, 512], P('ccd', 'exp')
Inputs may be any that keep to these rules, and one draw needn't show every extreme that they name: `sky_fibres`: 96 distinct fibre numbers, listed group by group: entries g * 6 to (g + 1) * 6 - 1 are fibres of the group g of 50 consecutive fibres. `fibre_slot`: for each group g of 50 consecutive fibres, a permutation of the slots g * 50 to (g + 1) * 50 - 1.
All inputs are finite; a program needn't handle non-finite values.
Results may differ from a plain program's by a relative error of at most 0.00095.
Values may be sent and summed in bfloat16 or wider, within the bound.
No kernel may reach another device: no remote copies, remote signals or barrier semaphores. Data moves between devices by JAX's collectives and lax.ppermute only.
A program may use at most 64 MiB of HBM per device.

v0:
```python
import jax
import jax.numpy as jnp
from jax import lax
from jax.sharding import PartitionSpec as P

BPIX = 500
MARG = 20
ROWS = 4
BAND = 11
SHIFT = 3
FC = 50
SPAN = 540
highest = lax.Precision.HIGHEST


def extended(x, sides, width):
    for axis, dim in sides:
        size, length = (lax.axis_size(axis), x.shape[dim])
        up = [(i, (i + 1) % size) for i in range(size - 1)]
        down = [(j, i) for i, j in up]
        last = lax.slice_in_dim(x, length - width, length, axis=dim)
        leading = lax.slice_in_dim(x, 0, width, axis=dim)
        before = lax.ppermute(last, axis, up)
        after = lax.ppermute(leading, axis, down)
        x = jnp.concatenate([before, x, after], axis=dim)
    return x


def band_model(pieces, spectra, shifts):
    length = pieces.shape[2]

    def window_of(shift):
        return lax.dynamic_slice(
            spectra, (jnp.int32(0), shift + SHIFT), (spectra.shape[0], length + BAND - 1)
        )

    windows = jax.vmap(window_of)(shifts)
    total = jnp.zeros((pieces.shape[0], spectra.shape[0], length), jnp.float32)
    for offset in range(BAND):
        total = total + pieces[:, offset, None, :] * windows[:, :, offset : offset + length]
    return total


def solve_small(gram, target):
    factor = jnp.linalg.cholesky(gram)
    return jax.scipy.linalg.cho_solve((factor, True), target[..., None])[..., 0]


def shards(pixels, psf_proj, resolution, basis, sky_fibres, fibre_slot, band_shift):
    padded = extended(pixels, (("ccd", 1),), MARG)
    pixvar = (0.25 + jnp.square(padded.astype(jnp.float32))).astype(jnp.bfloat16)
    proj_square = jnp.square(psf_proj.astype(jnp.float32)).astype(jnp.bfloat16)
    groups = pixels.shape[3]
    flux_parts = []
    var_parts = []
    for block in range(psf_proj.shape[0]):
        lower = block * BPIX
        window = padded[0, lower : lower + SPAN].reshape(SPAN * ROWS, groups)
        window_var = pixvar[0, lower : lower + SPAN].reshape(SPAN * ROWS, groups)
        flux_parts.append(jnp.dot(psf_proj[block], window, preferred_element_type=jnp.float32))
        var_parts.append(
            jnp.dot(proj_square[block], window_var, preferred_element_type=jnp.float32)
        )
    flux_slots = jnp.concatenate(flux_parts, 0).reshape(FC, ROWS * groups)
    var_slots = jnp.concatenate(var_parts, 0).reshape(FC, ROWS * groups)
    group_base = lax.axis_index("ccd") * FC
    local_slot = fibre_slot - group_base
    flux_rows = jnp.take(flux_slots, local_slot, axis=0)
    var_rows = jnp.take(var_slots, local_slot, axis=0)
    fibre_ids = group_base + jnp.arange(FC, dtype=jnp.int32)
    skymask = jnp.any(fibre_ids[:, None] == sky_fibres[None, :], axis=1).astype(jnp.float32)
    model = band_model(
        lax.all_gather(resolution.astype(jnp.bfloat16), "exp", axis=2, tiled=True).astype(
            jnp.float32
        ),
        basis,
        band_shift,
    )
    weight = skymask[:, None] / var_rows
    weighted = model * weight[:, None, :]
    gram = jnp.einsum("fkw,flw->kl", weighted, model, precision=highest)
    target = jnp.einsum("fkw,fw->k", weighted, flux_rows, precision=highest)
    gram, target = lax.psum((gram, target), "ccd")
    coeffs = solve_small(gram, target)
    residual = flux_rows - jnp.einsum("k,fkw->fw", coeffs, model, precision=highest)
    sky_subtracted = lax.all_to_all(residual[None], "exp", split_axis=2, concat_axis=0, tiled=True)
    centred = sky_subtracted - jnp.mean(sky_subtracted, axis=0)
    noise_rms = jnp.sqrt(jnp.mean(jnp.square(centred), axis=0) + 1e-06)
    return (sky_subtracted, noise_rms)


def solution(mesh):
    in_specs = (
        P("exp", "ccd", None, None),
        P("ccd", None, None),
        P("ccd", None, "exp"),
        P(),
        P(),
        P("ccd"),
        P("ccd"),
    )
    out_specs = (P(None, "ccd", "exp"), P("ccd", "exp"))
    return jax.shard_map(shards, mesh=mesh, in_specs=in_specs, out_specs=out_specs, check_vma=False)
```

profile of v0, /device:TPU:1, one launch (start us, length us, event | category | flops | bytes accessed | tf_op | source)
XLA Modules:
  0.0 216.6 jit_solution(9551410797200062274)
XLA Ops:
  0.6 1.4 fusion.23
  2.0 4.0 %collective-permute-start = (bf16[1,20,4,128]{3,2,1,0:T(4,128)(2,1)}, bf16[1,20,4,128]{3,2,1,0:T(4,128)(2,1)S(1)}, u32[]{:S(2)}, u32[]{:S(2)}) collective-permute-start(bf16[1,20,4,128]{3,2,1,0:T(4,128)(2,1)} %get-tuple-element.38), channel_id=1, source_target_pairs={{0,1},{1,2},{2,3},{3,4},{4,5},{5,6},{6,7},{7,8},{8,9},{9,10},{10,1... | collective-permute-start | bytes 61448 | tf_op jit(solution)/shard_map/ppermute | solution.py:23
  6.0 1.3 collective-permute-start.1
  7.4 0.9 convert_element_type.41
  8.3 45.0 %all_gather.3 = bf16[50,11,512]{0,2,1:T(8,128)(2,1)S(1)} all-gather(bf16[50,11,16]{0,2,1:T(8,128)(2,1)S(1)} %convert_element_type.41), channel_id=1, replica_groups=mesh['exp'=32,'ccd'=16] {'exp'}, dimensions={2}, use_global_device_ids=true | all-gather | bytes 580800 | tf_op jit(solution)/shard_map/all_gather | solution.py:73
  53.5 1.2 slice_bitcast_fusion.18
  54.7 1.1 copy.62
  55.8 1.7 copy.63
  57.5 1.7 copy.64
  59.2 1.7 copy.65
  60.9 1.7 copy.66
  62.6 1.7 copy.67
  68.9 61.5 %while.1 = (s32[]{:T(128)}, f32[10,528]{1,0:T(8,128)S(1)}, s32[50,2]{0,1:T(2,128)S(1)}, f32[50,10,522]{2,1,0:T(8,128)S(1)}, s32[]{:T(128)}) while((s32[]{:T(128)}, f32[10,528]{1,0:T(8,128)S(1)}, s32[50,2]{0,1:T(2,128)S(1)}, f32[50,10,522]{2,1,0:T(8,128)S(1)}, s32[]{:T(128)}) %tuple.39), condition=%wide.while_cond, body=%wide.while_body.sunk | while | flops 2 | bytes 82017 | solution.py:33
  130.5 1.4 multiply_convert_fusion
  132.2 6.5 %multiply_add_fusion = f32[50,10,512]{2,1,0:T(8,128)} fusion(f32[50,10,522]{2,1,0:T(8,128)S(1)} %get-tuple-element.10, f32[50,512]{1,0:T(8,128)S(1)} %copy-done.10, f32[50,512]{1,0:T(8,128)S(1)} %copy-done.9, f32[50,512]{1,0:T(8,128)S(1)} %copy-done.8, f32[50,512]{1,0:T(8,128)} %copy.69, f32[50,512]{1,0:T(8,128)} %copy.68, f32[50,512]{1,0:T(8,128)} %copy.67, ...), kind=kLoop, calls=%fused_computation.10 | loop fusion | flops 5376000 | bytes 13414400 | tf_op jit(solution)/shard_map/add | solution.py:40
  138.8 1.1 copy-done.1
  141.2 3.7 %add_convert_fusion = bf16[1,1040,4,128]{3,2,1,0:T(4,128)(2,1)S(1)} fusion(bf16[1,20,4,128]{3,2,1,0:T(4,128)(2,1)S(1)} %collective-permute-done.1, bf16[1,1000,4,128]{3,2,1,0:T(4,128)(2,1)S(1)} %copy-done.1, bf16[1,20,4,128]{3,2,1,0:T(4,128)(2,1)S(1)} %collective-permute-done), kind=kLoop, calls=%fused_computation.8 | loop fusion | flops 3194880 | bytes 2129920 | tf_op jit(solution)/shard_map/convert_element_type | solution.py:51
  147.4 2.3 %fusion.4 = f32[10,10]{0,1:T(8,128)S(1)} fusion(f32[50,10,512]{2,1,0:T(8,128)S(1)} %copy-done, f32[50,512]{1,0:T(8,128)S(1)} %get-tuple-element.41), kind=kOutput, calls=%fused_computation.13 | convolution fusion | flops 30976000 | bytes 1126800 | tf_op jit(solution)/shard_map/fkw,flw->kl/dot_general | solution.py:81
  149.7 2.0 fusion.7
  151.7 37.4 %all-reduce.1 = (f32[10,10]{0,1:T(8,128)S(1)}, f32[10]{0:T(128)S(1)}) all-reduce(f32[10,10]{0,1:T(8,128)S(1)} %fusion.4, f32[10]{0:T(128)S(1)} %fusion.7), channel_id=1, replica_groups=mesh['exp'=32,'ccd'=16] {'ccd'}, use_global_device_ids=true, to_apply=%region_1.3 | all-reduce | flops 110 | bytes 880 | tf_op jit(solution)/shard_map/psum | solution.py:83
  192.6 0.9 fusion.24
  194.2 1.3 reduce.7
  195.8 18.6 %all_to_all.18 = f32[32,1,800]{2,1,0:T(1,128)S(1)} all-to-all(f32[32,1,800]{2,1,0:T(1,128)S(1)} %reshape.151), channel_id=1, replica_groups=mesh['exp'=32,'ccd'=16] {'exp'}, dimensions={0} | all-to-all | bytes 204800 | tf_op jit(solution)/shard_map/all_to_all | solution.py:86
  214.4 0.9 reduce.8
  (223 shorter events, 75.8 us)
Async XLA Ops:
  2.0 136.8 %collective-permute-start = (bf16[1,20,4,128]{3,2,1,0:T(4,128)(2,1)}, bf16[1,20,4,128]{3,2,1,0:T(4,128)(2,1)S(1)}, u32[]{:S(2)}, u32[]{:S(2)}) collective-permute-start(bf16[1,20,4,128]{3,2,1,0:T(4,128)(2,1)} %get-tuple-element.38), channel_id=1, source_target_pairs={{0,1},{1,2},{2,3},{3,4},{4,5},{5,6},{6,7},{7,8},{8,9},{9,10},{10,1... | collective-permute-start | bytes 61448 | tf_op jit(solution)/shard_map/ppermute | solution.py:23
  6.0 132.7 %collective-permute-start.1 = (bf16[1,20,4,128]{3,2,1,0:T(4,128)(2,1)}, bf16[1,20,4,128]{3,2,1,0:T(4,128)(2,1)S(1)}, u32[]{:S(2)}, u32[]{:S(2)}) collective-permute-start(bf16[1,20,4,128]{3,2,1,0:T(4,128)(2,1)} %get-tuple-element.39), channel_id=1, source_target_pairs={{1,0},{2,1},{3,2},{4,3},{5,4},{6,5},{7,6},{8,7},{9,8},{10,9},{11,1... | collective-permute-start | bytes 61448 | tf_op jit(solution)/shard_map/ppermute | solution.py:24
  57.5 11.5 %copy-start.4 = (f32[10,528]{1,0:T(8,128)S(1)}, f32[10,528]{1,0:T(8,128)}, u32[]{:S(2)}) copy-start(f32[10,528]{1,0:T(8,128)} %param.12) | copy-start | bytes 63364
  65.2 65.3 %copy-start.11 = (s32[50]{0:T(128)S(1)}, s32[50]{0:T(128)}, u32[]{:S(2)}) copy-start(s32[50]{0:T(128)} %param.14) | copy-start | bytes 604
  66.7 65.2 %copy-start.12 = (s32[96]{0:T(128)S(1)}, s32[96]{0:T(128)}, u32[]{:S(2)}) copy-start(s32[96]{0:T(128)} %param.13) | copy-start | bytes 1156
  66.7 65.4 %copy-start.5 = (f32[50,512]{1,0:T(8,128)S(1)}, f32[50,512]{1,0:T(8,128)}, u32[]{:S(2)}) copy-start(f32[50,512]{1,0:T(8,128)} %copy.63) | copy-start | bytes 307204
  66.7 65.4 %copy-start.6 = (f32[50,512]{1,0:T(8,128)S(1)}, f32[50,512]{1,0:T(8,128)}, u32[]{:S(2)}) copy-start(f32[50,512]{1,0:T(8,128)} %copy.64) | copy-start | bytes 307204
  66.7 65.4 %copy-start.7 = (f32[50,512]{1,0:T(8,128)S(1)}, f32[50,512]{1,0:T(8,128)}, u32[]{:S(2)}) copy-start(f32[50,512]{1,0:T(8,128)} %copy.65) | copy-start | bytes 307204
  130.5 1.7 copy-start.8
  130.5 1.7 copy-start.9
  130.5 1.7 copy-start.10
  132.2 6.5 %copy-start.2 = (bf16[2,100,2160]{2,0,1:T(2,128)(2,1)S(1)}, bf16[2,100,2160]{2,0,1:T(2,128)(2,1)}, u32[]{:S(2)}) copy-start(bf16[2,100,2160]{2,0,1:T(2,128)(2,1)} %param.10) | copy-start | bytes 2592004
  138.6 1.2 copy-start.1
  145.9 1.4 copy-start
  215.9 0.7 copy-start.3
where the time goes:
time: 220 us; the launch traced here: 217 us
  blocking collectives  101 us (46%)
  local copies, waits for them, and re-layouts  82 us (37%)
  other arithmetic  20.4 us (9%)
  matrix products  6.68 us (3%)
  starting transfers between devices  5.31 us (2%)
    gather x150, local copies, waits for them, and re-layouts  61.4 us
    all_gather x1, blocking collectives, shards(): lax.all_gather(resolution.astype(jnp.bfloat16), 'exp', axis=2, tiled=True)  45 us
    psum x1, blocking collectives, shards(): gram, target = lax.psum((gram, target), 'ccd')  37.4 us
    all_to_all x1, blocking collectives, shards(): lax.all_to_all(residual[None], 'exp', split_axis=2, concat_axis=0, tiled=...  18.6 us
    mul x12, local copies, waits for them, and re-layouts, band_model(): pieces[:, offset, None, :] * windows[:, :, offset:offset + length]  14.7 us
    add x1, other arithmetic, band_model(): total + pieces[:, offset, None, :] * windows[:, :, offset:offset + length]  6.47 us
  transfers between devices with their start and end apart: 2, of which 0 were waited for; matrix products, arithmetic and copies ran while one was open for 40% of the time, Pallas kernels for 0%

commit v1 on v0

--- a/solution.py
+++ b/solution.py
@@ -70,9 +70,12 @@
     fibre_ids = group_base + jnp.arange(FC, dtype=jnp.int32)
     skymask = jnp.any(fibre_ids[:, None] == sky_fibres[None, :], axis=1).astype(jnp.float32)
     model = band_model(
-        lax.all_gather(resolution.astype(jnp.bfloat16), "exp", axis=2, tiled=True).astype(
-            jnp.float32
-        ),
+        jnp.concatenate(
+            lax.all_to_all(
+                jnp.stack([resolution.astype(jnp.bfloat16)] * lax.axis_size("exp")), "exp", 0, 0
+            ),
+            axis=2,
+        ).astype(jnp.float32),
         basis,
         band_shift,
     )

time: 220 us -> 199 us (0.905); the launches traced: 217 us -> 198 us
  blocking collectives: 101 us -> 60.8 us
  starting transfers between devices: 5.31 us -> 17.8 us
  local copies, waits for them, and re-layouts: 82 us -> 89.4 us
    all_gather x1 -> x0, blocking collectives: 45 us -> none  [shards(): lax.all_gather(resolution.astype(jnp.bfloat16), 'exp', axis=2, tiled=True)]
    all_to_all x0 -> x1, starting transfers between devices: none -> 13.1 us  [shards(): lax.all_to_all(jnp.stack([resolution.astype(jnp.bfloat16)] * lax.axis_siz...]
    unnamed x30 -> x33, local copies, waits for them, and re-layouts: 2.53 us -> 9.32 us
    all_to_all x1, blocking collectives: 18.6 us -> 24 us  [shards(): lax.all_to_all(residual[None], 'exp', split_axis=2, concat_axis=0, tiled=...]
    gather x150, local copies, waits for them, and re-layouts: 61.4 us -> 65.8 us
    mul x12, local copies, waits for them, and re-layouts: 14.7 us -> 12.1 us  [band_model(): pieces[:, offset, None, :] * windows[:, :, offset:offset + length]]
  transfers between devices with their start and end apart: 2 -> 3, of which waited for: 0 -> 0; matrix products, arithmetic and copies ran while one was open for 40% -> 39% of each run, Pallas kernels for 0% -> 0%
where the time goes in v1:
time: 199 us; the launch traced here: 198 us
  local copies, waits for them, and re-layouts  89.4 us (45%)
  blocking collectives  60.8 us (31%)
  other arithmetic  20.7 us (10%)
  starting transfers between devices  17.8 us (9%)
  matrix products  8.08 us (4%)
    gather x150, local copies, waits for them, and re-layouts  65.8 us
    psum x1, blocking collectives, shards(): gram, target = lax.psum((gram, target), 'ccd')  36.8 us
    all_to_all x1, blocking collectives, shards(): lax.all_to_all(residual[None], 'exp', split_axis=2, concat_axis=0, tiled=...  24 us
    all_to_all x1, starting transfers between devices, shards(): lax.all_to_all(jnp.stack([resolution.astype(jnp.bfloat16)] * lax.axis_siz...  13.1 us
    mul x12, local copies, waits for them, and re-layouts, band_model(): pieces[:, offset, None, :] * windows[:, :, offset:offset + length]  12.1 us
    unnamed x33, local copies, waits for them, and re-layouts  9.32 us
    add x1, other arithmetic, band_model(): total + pieces[:, offset, None, :] * windows[:, :, offset:offset + length]  5.82 us
  transfers between devices with their start and end apart: 3, of which 0 were waited for; matrix products, arithmetic and copies ran while one was open for 39% of the time, Pallas kernels for 0%

profile of v1, /device:TPU:1, one launch (start us, length us, event | category | flops | bytes accessed | tf_op | source)
XLA Modules:
  0.0 198.0 jit_solution(3949466347977027966)
XLA Ops:
  0.6 0.9 convert_element_type.47
  1.8 3.2 %reshape.158 = bf16[32,2,4400]{2,1,0:T(2,128)(2,1)} reshape(bf16[32,11,16,50]{3,2,1,0:T(8,128)(2,1)S(1)} %broadcast_bitcast_fusion) | data formatting | bytes 1126400
  5.0 13.1 %all-to-all-start = ((bf16[32,2,4400]{2,1,0:T(2,128)(2,1)}), bf16[32,2,4400]{2,1,0:T(2,128)(2,1)}, u32[]{:S(2)}, u32[]{:S(2)}) async-start(bf16[32,2,4400]{2,1,0:T(2,128)(2,1)} %reshape.158), calls=%async_computation | async-start | bytes 1146880 | tf_op jit(solution)/shard_map/all_to_all | solution.py:74
  18.1 3.2 %collective-permute-start = (bf16[1,20,4,128]{3,2,1,0:T(4,128)(2,1)S(1)}, bf16[1,20,4,128]{3,2,1,0:T(4,128)(2,1)S(1)}, u32[]{:S(2)}, u32[]{:S(2)}) collective-permute-start(bf16[1,20,4,128]{3,2,1,0:T(4,128)(2,1)S(1)} %get-tuple-element.38), channel_id=1, source_target_pairs={{0,1},{1,2},{2,3},{3,4},{4,5},{5,6},{6,7},{7,8},{8,9},{9,10},{10,1... | collective-permute-start | bytes 61448 | tf_op jit(solution)/shard_map/ppermute | solution.py:23
  21.3 1.5 collective-permute-start.1
  22.9 65.9 %while.1 = (s32[]{:T(128)}, f32[10,528]{1,0:T(8,128)S(1)}, s32[50,2]{0,1:T(2,128)S(1)}, f32[50,10,522]{2,1,0:T(8,128)S(1)}, s32[]{:T(128)}) while((s32[]{:T(128)}, f32[10,528]{1,0:T(8,128)S(1)}, s32[50,2]{0,1:T(2,128)S(1)}, f32[50,10,522]{2,1,0:T(8,128)S(1)}, s32[]{:T(128)}) %tuple.39), condition=%wide.while_cond, body=%wide.while_body.sunk | while | flops 2 | bytes 82017 | solution.py:33
  88.7 2.3 %multiply_convert_fusion = bf16[2,100,2160]{2,1,0:T(8,128)(2,1)} fusion(bf16[2,100,2160]{2,0,1:T(2,128)(2,1)} %param.10), kind=kLoop, calls=%fused_computation.10 | loop fusion | flops 1296000 | bytes 1728000 | tf_op jit(solution)/shard_map/convert_element_type | solution.py:52
  92.8 3.7 %add_convert_fusion = bf16[1,1040,4,128]{3,2,1,0:T(4,128)(2,1)S(1)} fusion(bf16[1,20,4,128]{3,2,1,0:T(4,128)(2,1)S(1)} %collective-permute-done.1, bf16[1,1000,4,128]{3,2,1,0:T(4,128)(2,1)S(1)} %copy-done.1, bf16[1,20,4,128]{3,2,1,0:T(4,128)(2,1)S(1)} %collective-permute-done), kind=kLoop, calls=%fused_computation.9 | loop fusion | flops 3194880 | bytes 2129920 | tf_op jit(solution)/shard_map/convert_element_type | solution.py:51
  100.4 3.7 %reshape.159 = bf16[32,11,16,50]{3,2,1,0:T(8,128)(2,1)S(1)} reshape(bf16[32,2,4400]{2,1,0:T(2,128)(2,1)} %all-to-all-done) | data formatting | bytes 1126400
  104.5 1.2 slice_bitcast_fusion.18
  105.7 1.1 copy.54
  106.8 1.7 copy.55
  108.5 1.7 copy.56
  110.2 1.7 copy.57
  112.0 1.7 copy.58
  113.7 1.7 copy.59
  116.7 5.8 %multiply_add_fusion = f32[50,10,512]{2,1,0:T(8,128)S(1)} fusion(f32[50,10,522]{2,1,0:T(8,128)S(1)} %get-tuple-element.10, f32[50,512]{1,0:T(8,128)S(1)} %copy.64, f32[50,512]{1,0:T(8,128)S(1)} %copy.63, f32[50,512]{1,0:T(8,128)S(1)} %copy.62, f32[50,512]{1,0:T(8,128)S(1)} %copy.61, f32[50,512]{1,0:T(8,128)} %copy.60, f32[50,512]{1,0:T(8,128)} %copy.59, ...), kind=kLoop, calls=%fused_computation.11 | loop fusion | flops 5376000 | bytes 13414400 | tf_op jit(solution)/shard_map/add | solution.py:40
  122.6 2.3 %fusion.4 = f32[10,10]{0,1:T(8,128)S(1)} fusion(f32[50,10,512]{2,1,0:T(8,128)S(1)} %multiply_add_fusion, f32[50,512]{1,0:T(8,128)S(1)} %copy-done.7), kind=kOutput, calls=%fused_computation.14 | convolution fusion | flops 30976000 | bytes 1126800 | tf_op jit(solution)/shard_map/fkw,flw->kl/dot_general | solution.py:84
  124.9 2.0 %fusion.7 = f32[10]{0:T(128)S(1)} fusion(f32[50,10,512]{2,1,0:T(8,128)S(1)} %multiply_add_fusion, f32[50,512]{1,0:T(8,128)S(1)} %copy-done.7, f32[50,512,1]{1,0,2:T(8,128)S(1)} %copy-done.9), kind=kOutput, calls=%fused_computation.15 | convolution fusion | flops 3328000 | bytes 1228840 | tf_op jit(solution)/shard_map/fkw,fw->k/dot_general | solution.py:85
  126.9 36.8 %all-reduce.1 = (f32[10,10]{0,1:T(8,128)S(1)}, f32[10]{0:T(128)S(1)}) all-reduce(f32[10,10]{0,1:T(8,128)S(1)} %fusion.4, f32[10]{0:T(128)S(1)} %fusion.7), channel_id=1, replica_groups=mesh['exp'=32,'ccd'=16] {'ccd'}, use_global_device_ids=true, to_apply=%region_1.3 | all-reduce | flops 110 | bytes 880 | tf_op jit(solution)/shard_map/psum | solution.py:86
  167.1 2.3 %fusion.24 = f32[1,50,512]{2,0,1:T(1,128)S(1)} fusion(f32[10,1,1]{0,1,2:T(1,128)S(1)} %convolution_bitcast_fusion.2, f32[50,10,512]{2,1,0:T(8,128)} %copy-done), kind=kOutput, calls=%fused_computation.70 | convolution fusion | flops 3072000 | bytes 1126440 | tf_op jit(solution)/shard_map/k,fkw->fw/dot_general | solution.py:88
  170.2 1.3 reduce.7
  171.8 24.0 %all_to_all.23 = f32[32,1,800]{2,1,0:T(1,128)S(1)} all-to-all(f32[32,1,800]{2,1,0:T(1,128)S(1)} %reshape.160), channel_id=1, replica_groups=mesh['exp'=32,'ccd'=16] {'exp'}, dimensions={0} | all-to-all | bytes 204800 | tf_op jit(solution)/shard_map/all_to_all | solution.py:89
  195.8 0.9 reduce.8
  (228 shorter events, 78.9 us)
Async XLA Ops:
  1.7 16.4 %copy-start.1 = (bf16[1,1000,4,128]{3,2,1,0:T(4,128)(2,1)S(1)}, bf16[1,1000,4,128]{3,2,1,0:T(4,128)(2,1)}, u32[]{:S(2)}) copy-start(bf16[1,1000,4,128]{3,2,1,0:T(4,128)(2,1)} %param.9) | copy-start | bytes 3072004
  1.7 21.1 %copy-start.11 = (s32[50]{0:T(128)S(1)}, s32[50]{0:T(128)}, u32[]{:S(2)}) copy-start(s32[50]{0:T(128)} %param.15) | copy-start | bytes 604
  1.7 21.1 %copy-start.8 = (f32[10,528]{1,0:T(8,128)S(1)}, f32[10,528]{1,0:T(8,128)}, u32[]{:S(2)}) copy-start(f32[10,528]{1,0:T(8,128)} %param.12) | copy-start | bytes 63364
  1.8 87.0 %copy-start.10 = (s32[50]{0:T(128)S(1)}, s32[50]{0:T(128)}, u32[]{:S(2)}) copy-start(s32[50]{0:T(128)} %param.14) | copy-start | bytes 604
  5.0 86.1 %copy-start.12 = (s32[96]{0:T(128)S(1)}, s32[96]{0:T(128)}, u32[]{:S(2)}) copy-start(s32[96]{0:T(128)} %param.13) | copy-start | bytes 1156
  5.0 95.4 %all-to-all-start = ((bf16[32,2,4400]{2,1,0:T(2,128)(2,1)}), bf16[32,2,4400]{2,1,0:T(2,128)(2,1)}, u32[]{:S(2)}, u32[]{:S(2)}) async-start(bf16[32,2,4400]{2,1,0:T(2,128)(2,1)} %reshape.158), calls=%async_computation | async-start | bytes 1146880 | tf_op jit(solution)/shard_map/all_to_all | solution.py:74
  18.1 73.3 %collective-permute-start = (bf16[1,20,4,128]{3,2,1,0:T(4,128)(2,1)S(1)}, bf16[1,20,4,128]{3,2,1,0:T(4,128)(2,1)S(1)}, u32[]{:S(2)}, u32[]{:S(2)}) collective-permute-start(bf16[1,20,4,128]{3,2,1,0:T(4,128)(2,1)S(1)} %get-tuple-element.38), channel_id=1, source_target_pairs={{0,1},{1,2},{2,3},{3,4},{4,5},{5,6},{6,7},{7,8},{8,9},{9,10},{10,1... | collective-permute-start | bytes 61448 | tf_op jit(solution)/shard_map/ppermute | solution.py:23
  21.3 70.1 %collective-permute-start.1 = (bf16[1,20,4,128]{3,2,1,0:T(4,128)(2,1)S(1)}, bf16[1,20,4,128]{3,2,1,0:T(4,128)(2,1)S(1)}, u32[]{:S(2)}, u32[]{:S(2)}) collective-permute-start(bf16[1,20,4,128]{3,2,1,0:T(4,128)(2,1)S(1)} %get-tuple-element.39), channel_id=1, source_target_pairs={{1,0},{2,1},{3,2},{4,3},{5,4},{6,5},{7,6},{8,7},{9,8},{10,9},{11,1... | collective-permute-start | bytes 61448 | tf_op jit(solution)/shard_map/ppermute | solution.py:24
  88.7 2.6 %copy-start.3 = (bf16[2,100,2160]{2,0,1:T(2,128)(2,1)S(1)}, bf16[2,100,2160]{2,0,1:T(2,128)(2,1)}, u32[]{:S(2)}) copy-start(bf16[2,100,2160]{2,0,1:T(2,128)(2,1)} %param.10) | copy-start | bytes 2592004
  96.5 1.2 copy-start.2
  98.9 1.4 copy-start.5
  116.7 5.8 %copy-start.7 = (f32[50,512]{1,0:T(8,128)S(1)}, f32[50,512]{1,0:T(8,128)}, u32[]{:S(2)}) copy-start(f32[50,512]{1,0:T(8,128)} %get-tuple-element.41) | copy-start | bytes 307204
  122.5 2.3 %copy-start = (f32[50,10,512]{2,1,0:T(8,128)}, f32[50,10,512]{2,1,0:T(8,128)S(1)}, u32[]{:S(2)}) copy-start(f32[50,10,512]{2,1,0:T(8,128)S(1)} %multiply_add_fusion) | copy-start | bytes 3072004
  122.5 2.3 %copy-start.9 = (f32[50,512,1]{1,0,2:T(8,128)S(1)}, f32[50,512,1]{1,0,2:T(8,128)}, u32[]{:S(2)}) copy-start(f32[50,512,1]{1,0,2:T(8,128)} %get-tuple-element.40) | copy-start | bytes 307204
  124.9 44.6 %copy-start.6 = (f32[50,512]{1,0:T(8,128)S(1)}, f32[50,512]{1,0:T(8,128)}, u32[]{:S(2)}) copy-start(f32[50,512]{1,0:T(8,128)} %copy-done.5) | copy-start | bytes 307204
  197.3 0.7 copy-start.4
